TPU v7x, 32 devices: a whole 2x2x4 slice. The times are simulated.
32 devices in a mesh: dp: 16 (over z, x, core), mp: 2 (over y).
Axes of the slice: x: 2, y: 2, z: 4, core: 2. Of those that a mesh axis runs over, the one named last changes fastest.
Arguments:
- frames_in: float32 [12288, 768], P(('dp', 'mp')), may hold values from -6 to 6
- frames_cot: float32 [12288, 768], P(('dp', 'mp')), may hold values from -6 to 6
- clip_ids: int32 [12288], replicated, may hold values from 0 to 16, never falling along the last dimension, each value on 1 to 768 neighbouring positions
- frame_mask: int32 [12288], replicated, may hold values 0 or 1
- norm_gain: float32 [2, 2, 768], replicated, may hold values from 0.25 to 1.75
- norm_bias: float32 [2, 2, 768], replicated, may hold values from -2 to 2
- qkv_weight: bfloat16 [2, 768, 3, 768], P(None, 'dp', None, 'mp'), as said below
- qv_bias: float32 [2, 2, 768], P(None, None, 'mp'), may hold values from -0.4 to 0.4
- proj_weight: bfloat16 [2, 768, 768], P(None, ('mp', 'dp')), may hold values from -4 to 4
- up_weight: bfloat16 [2, 768, 3072], P(None, 'dp', 'mp'), may hold values from -0.21875 to 0.21875
- up_bias: float32 [2, 3072], P(None, 'mp'), may hold values from -3 to 3
- down_weight: bfloat16 [2, 3072, 768], P(None, ('mp', 'dp')), may hold values from -0.109375 to 0.109375
- out_biases: float32 [2, 2, 768], replicated, may hold values from -2 to 2
Outputs:
- frames_out: float32 [12288, 768], P(('dp', 'mp'))
- frames_grad: float32 [12288, 768], P(('dp', 'mp'))
- grad_qkv: float32 [2, 768, 3, 768], P(None, 'dp', None, 'mp')
- grad_qv_bias: float32 [2, 2, 768], P(None, None, 'mp')
- grad_proj: float32 [2, 768, 768], P(None, ('mp', 'dp'))
- grad_up: float32 [2, 768, 3072], P(None, 'dp', 'mp')
- grad_up_bias: float32 [2, 3072], P(None, 'mp')
- grad_down: float32 [2, 3072, 768], P(None, ('mp', 'dp'))
- grad_gain: float32 [2, 2, 768], replicated
- grad_norm_bias: float32 [2, 2, 768], replicated
- grad_out_biases: float32 [2, 2, 768], replicated
Inputs may be any that keep to these rules, and one draw needn't show every extreme that they name: `clip_ids`: clip numbers never fall from one frame to the next; each clip holds 1 to 768 frames and one holds exactly 768. `qkv_weight`: projection weights for queries, keys and values.
All inputs are finite; a program needn't handle non-finite values.
Results may differ from a plain program's by a relative error of at most 0.013.
Values may be sent and summed in bfloat16 or wider, within the bound.
A program may use at most 320 MiB of HBM per device.

v0:
```python
import jax
import jax.numpy as jnp
from jax import lax
from jax.sharding import PartitionSpec as P

HD = 64
epsilon = 1e-05


def padded_2(block, sides, width):
    for axis, dim in sides:
        count = lax.axis_size(axis)
        forward = [(i, i + 1) for i in range(count - 1)]
        backward = [(target, source) for source, target in forward]
        low = lax.ppermute(
            lax.slice_in_dim(block, block.shape[dim] - width, None, axis=dim), axis, forward
        )
        high = lax.ppermute(lax.slice_in_dim(block, 0, width, axis=dim), axis, backward)
        block = jnp.concatenate([low, block, high], axis=dim)
    return block


def shifted(x, axis, by):
    size = lax.axis_size(axis)
    pairs = [(i, i + by) for i in range(size) if 0 <= i + by < size]
    return lax.ppermute(x, axis, pairs)


def norm_forward(values, gain_vec, bias_vec):
    row_mean = jnp.mean(values, axis=-1, keepdims=True)
    centred = values - row_mean
    inverse = lax.rsqrt(jnp.mean(centred * centred, axis=-1, keepdims=True) + epsilon)
    normed = centred * inverse
    return ((normed * gain_vec + bias_vec).astype(jnp.bfloat16), normed, inverse)


def norm_backward(grad_out, normed, inverse, gain_vec):
    scaled = grad_out * gain_vec
    projected = (
        scaled
        - jnp.mean(scaled, axis=-1, keepdims=True)
        - normed * jnp.mean(scaled * normed, axis=-1, keepdims=True)
    )
    return (inverse * projected, jnp.sum(grad_out * normed, axis=0), jnp.sum(grad_out, axis=0))


def gelu_value(preact):
    return 0.5 * preact * (1.0 + jax.scipy.special.erf(preact * 0.7071067811865476))


def gelu_slope(preact):
    return (
        0.5 * (1.0 + jax.scipy.special.erf(preact * 0.7071067811865476))
        + preact * jnp.exp(-0.5 * preact * preact) * 0.3989422804014327
    )


def padded(values, tok_span, fill):
    border = jnp.full((tok_span,) + values.shape[1:], fill, values.dtype)
    return jnp.concatenate([border, values, border], axis=0)


def block_mask(query_ids, block_start, key_ids, key_valid, tok_span):
    query_pos = block_start + jnp.arange(query_ids.shape[0], dtype=jnp.int32)
    key_pos = jnp.arange(key_ids.shape[0], dtype=jnp.int32)
    same_clip = query_ids[:, None] == key_ids[None, :]
    visible = (key_valid[None, :] == 1) | (key_pos[None, :] == query_pos[:, None] + tok_span)
    return same_clip & visible


def window_ids(clip_ids, frame_mask, tok_span):
    offset = lax.axis_index("dp") * tok_span
    ids_pad = padded(clip_ids, tok_span, -1)
    valid_pad = padded(frame_mask, tok_span, 0)
    return (
        lax.dynamic_slice_in_dim(ids_pad, offset + tok_span, tok_span, 0),
        lax.dynamic_slice_in_dim(ids_pad, offset, 3 * tok_span, 0),
        lax.dynamic_slice_in_dim(valid_pad, offset, 3 * tok_span, 0),
    )


def fetch_weights(qkv_weight, proj_weight, up_weight, down_weight, depth):
    return (
        lax.all_gather(qkv_weight[depth], "dp", axis=0, tiled=True),
        lax.all_gather(proj_weight[depth], "dp", axis=0, tiled=True),
        lax.all_gather(up_weight[depth], "dp", axis=0, tiled=True),
        lax.all_gather(down_weight[depth], "dp", axis=0, tiled=True),
    )


def gather_rows(values):
    return lax.all_gather(values, "mp", axis=0, tiled=True)


def sum_rows(left, right):
    return lax.psum_scatter(
        jnp.dot(left, right, preferred_element_type=jnp.float32),
        "mp",
        scatter_dimension=0,
        tiled=True,
    )


def block_scores(query, keys, query_ids, key_ids, key_valid, offset):
    tok_span = query.shape[0]
    allowed = block_mask(query_ids, offset, key_ids, key_valid, tok_span)
    scores = jnp.einsum("qhd,khd->hqk", query, keys, preferred_element_type=jnp.float32) * HD ** (
        -0.5
    )
    return (query, jnp.where(allowed[None], scores, -1e30))


def attend(query, key_vals, query_ids, key_ids, key_valid):
    tok_span = query.shape[0]
    n_blocks = (tok_span + 1023) // 1024
    block_rows = tok_span // n_blocks
    keys = key_vals[:, 0]
    values = key_vals[:, 1]

    def one_block(block_id):
        offset = block_id * block_rows
        query_block, scores = block_scores(query, keys, query_ids, key_ids, key_valid, offset)
        row_max = jnp.max(scores, axis=-1, keepdims=True)
        log_total = row_max + jnp.log(jnp.sum(jnp.exp(scores - row_max), axis=-1, keepdims=True))
        prob_low = jnp.exp(scores - log_total).astype(jnp.bfloat16)
        attended = jnp.einsum(
            "hqk,khd->qhd", prob_low, values, preferred_element_type=jnp.float32
        ).astype(jnp.bfloat16)
        return (attended, log_total[..., 0])

    attended, log_totals = lax.map(one_block, jnp.arange(n_blocks, dtype=jnp.int32))
    return (attended.reshape(query.shape), log_totals)


def attend_back(query, key_vals, attended, grad_attn, log_totals, query_ids, key_ids, key_valid):
    tok_span = query.shape[0]
    n_blocks = (tok_span + 1023) // 1024
    block_rows = tok_span // n_blocks
    score_scale = HD ** (-0.5)
    keys = key_vals[:, 0]
    values = key_vals[:, 1]

    def one_block(key_grads, block_id):
        offset = block_id * block_rows
        query_block, scores = block_scores(query, keys, query_ids, key_ids, key_valid, offset)
        prob_full = jnp.exp(scores - log_totals[block_id][..., None])
        prob_low = prob_full.astype(jnp.bfloat16)
        grad_prob = jnp.einsum(
            "qhd,khd->hqk", grad_attn, values, preferred_element_type=jnp.float32
        )
        delta_row = jnp.sum(grad_attn.astype(jnp.float32) * attended.astype(jnp.float32), axis=-1).T
        score_low = (prob_full * (grad_prob - delta_row[..., None])).astype(jnp.bfloat16)
        grad_query = (
            jnp.einsum("hqk,khd->qhd", score_low, keys, preferred_element_type=jnp.float32)
            * score_scale
        )
        grad_key = (
            jnp.einsum("hqk,qhd->khd", score_low, query_block, preferred_element_type=jnp.float32)
            * score_scale
        )
        grad_value = jnp.einsum(
            "hqk,qhd->khd", prob_low, grad_attn, preferred_element_type=jnp.float32
        )
        return (key_grads + jnp.stack([grad_key, grad_value], axis=1), grad_query)

    start = jnp.zeros((3 * tok_span, 2) + query.shape[1:], jnp.float32)
    key_grads, grad_query = lax.scan(one_block, start, jnp.arange(n_blocks, dtype=jnp.int32))
    return (grad_query.reshape(query.shape), key_grads)


def widen(piece, full_width, mp_index):
    out_shape = piece.shape[:-1] + (full_width,)
    return lax.dynamic_update_slice_in_dim(
        jnp.zeros(out_shape, jnp.float32), piece, mp_index * piece.shape[-1], piece.ndim - 1
    )


def layer_forward(
    state, matrices, gain_pair, bias_pair, qv_pair, up_vec, out_pair, query_ids, key_ids, key_valid
):
    qkv_mat, proj_mat, up_mat, down_mat = matrices
    head_cols = qkv_mat.shape[-1]
    first_norm, hat_one, inv_one = norm_forward(state, gain_pair[0], bias_pair[0])
    first_full = gather_rows(first_norm)
    tok_span = first_full.shape[0]
    bias_three = jnp.stack([qv_pair[0], jnp.zeros_like(qv_pair[0]), qv_pair[1]])
    qkv_proj = jnp.dot(
        first_full,
        qkv_mat.reshape(qkv_mat.shape[0], 3 * head_cols),
        preferred_element_type=jnp.float32,
    )
    qkv_proj = (qkv_proj.reshape(tok_span, 3, head_cols) + bias_three).astype(jnp.bfloat16)
    query = qkv_proj[:, 0].reshape(tok_span, head_cols // HD, HD)
    key_vals = qkv_proj[:, 1:].reshape(tok_span, 2 * head_cols)
    key_vals = padded_2(key_vals, (("dp", 0),), tok_span)
    key_vals = key_vals.reshape(3 * tok_span, 2, head_cols // HD, HD)
    attended, log_totals = attend(query, key_vals, query_ids, key_ids, key_valid)
    attn_flat = attended.reshape(tok_span, head_cols)
    middle = state + sum_rows(attn_flat, proj_mat) + out_pair[0]
    second_norm, hat_two, inv_two = norm_forward(middle, gain_pair[1], bias_pair[1])
    second_full = gather_rows(second_norm)
    preact = jnp.dot(second_full, up_mat, preferred_element_type=jnp.float32) + up_vec
    hidden = gelu_value(preact).astype(jnp.bfloat16)
    result = middle + sum_rows(hidden, down_mat) + out_pair[1]
    stored = {
        "hat_one": hat_one,
        "inv_one": inv_one,
        "first_full": first_full,
        "query": query,
        "key_vals": key_vals,
        "attended": attended,
        "log_totals": log_totals,
        "hat_two": hat_two,
        "inv_two": inv_two,
        "second_full": second_full,
        "preact": preact,
        "hidden": hidden,
    }
    return (stored, result)


def layer_backward(gradient, stored, matrices, gain_pair, query_ids, key_ids, key_valid):
    qkv_mat, proj_mat, up_mat, down_mat = matrices
    head_cols = qkv_mat.shape[-1]
    grad_full = gather_rows(gradient.astype(jnp.bfloat16))
    grad_down = jnp.dot(stored["hidden"].T, grad_full, preferred_element_type=jnp.float32)
    grad_pre = jnp.dot(grad_full, down_mat.T, preferred_element_type=jnp.float32) * gelu_slope(
        stored["preact"]
    )
    grad_upb = jnp.sum(grad_pre, axis=0)
    pre_low = grad_pre.astype(jnp.bfloat16)
    grad_up = jnp.dot(stored["second_full"].T, pre_low, preferred_element_type=jnp.float32)
    grad_second = sum_rows(pre_low, up_mat.T)
    back_two, gain_two, shift_two = norm_backward(
        grad_second, stored["hat_two"], stored["inv_two"], gain_pair[1]
    )
    grad_middle = gradient + back_two
    middle_full = gather_rows(grad_middle.astype(jnp.bfloat16))
    attended = stored["attended"]
    tok_span = attended.shape[0]
    grad_proj = jnp.dot(
        attended.reshape(tok_span, head_cols).T, middle_full, preferred_element_type=jnp.float32
    )
    grad_attn = jnp.dot(middle_full, proj_mat.T, preferred_element_type=jnp.float32).astype(
        jnp.bfloat16
    )
    grad_attn = grad_attn.reshape(attended.shape)
    grad_query, key_grads = attend_back(
        stored["query"],
        stored["key_vals"],
        attended,
        grad_attn,
        stored["log_totals"],
        query_ids,
        key_ids,
        key_valid,
    )
    key_grads = key_grads.reshape(3 * tok_span, 2 * head_cols)
    own_grads = key_grads[tok_span : 2 * tok_span]
    for step_by, piece in ((1, key_grads[2 * tok_span :]), (-1, key_grads[:tok_span])):
        own_grads = own_grads + shifted(piece.astype(jnp.bfloat16), "dp", step_by).astype(
            piece.dtype
        )
    grad_query = grad_query.reshape(tok_span, head_cols)
    grad_key = own_grads[:, :head_cols]
    grad_value = own_grads[:, head_cols:]
    grad_qv = jnp.stack([jnp.sum(grad_query, axis=0), jnp.sum(grad_value, axis=0)])
    qkv_low = (
        jnp.stack([grad_query, grad_key, grad_value], axis=1)
        .astype(jnp.bfloat16)
        .reshape(tok_span, 3 * head_cols)
    )
    grad_qkv = jnp.dot(stored["first_full"].T, qkv_low, preferred_element_type=jnp.float32).reshape(
        -1, 3, head_cols
    )
    grad_first = sum_rows(qkv_low, qkv_mat.reshape(-1, 3 * head_cols).T)
    back_one, gain_one, shift_one = norm_backward(
        grad_first, stored["hat_one"], stored["inv_one"], gain_pair[0]
    )
    new_grad = grad_middle + back_one
    mp_index = lax.axis_index("mp")
    mp_count = lax.axis_size("mp")
    small = (
        jnp.stack([gain_one, gain_two]),
        jnp.stack([shift_one, shift_two]),
        jnp.stack([jnp.sum(grad_middle, axis=0), jnp.sum(gradient, axis=0)]),
        widen(grad_qv, head_cols * mp_count, mp_index),
        widen(grad_upb, grad_upb.shape[0] * mp_count, mp_index),
    )
    return (new_grad, (grad_qkv, grad_proj, grad_up, grad_down), small)


def body(
    frames_in,
    frames_cot,
    clip_ids,
    frame_mask,
    norm_gain,
    norm_bias,
    qkv_weight,
    qv_bias,
    proj_weight,
    up_weight,
    up_bias,
    down_weight,
    out_biases,
):
    layers = qkv_weight.shape[0]
    tok_span = frames_in.shape[0] * lax.axis_size("mp")
    query_ids, key_ids, key_valid = window_ids(clip_ids, frame_mask, tok_span)
    stored_all = []
    state = frames_in
    for depth in range(layers):
        matrices = fetch_weights(qkv_weight, proj_weight, up_weight, down_weight, depth)
        stored, state = layer_forward(
            state,
            matrices,
            norm_gain[depth],
            norm_bias[depth],
            qv_bias[depth],
            up_bias[depth],
            out_biases[depth],
            query_ids,
            key_ids,
            key_valid,
        )
        stored_all.append(stored)
    gradient = frames_cot
    weight_grads = []
    small_grads = []
    for depth in range(layers - 1, -1, -1):
        matrices = fetch_weights(qkv_weight, proj_weight, up_weight, down_weight, depth)
        gradient, mats_grad, small = layer_backward(
            gradient, stored_all[depth], matrices, norm_gain[depth], query_ids, key_ids, key_valid
        )
        mats_grad = (
            lax.psum_scatter(mats_grad[0], "dp", scatter_dimension=0, tiled=True),
            lax.psum_scatter(mats_grad[1], "dp", scatter_dimension=0, tiled=True),
            lax.psum_scatter(mats_grad[2], "dp", scatter_dimension=0, tiled=True),
            lax.psum_scatter(mats_grad[3], "dp", scatter_dimension=0, tiled=True),
        )
        small = lax.psum((small[0], small[1], small[2], small[3], small[4]), ("dp", "mp"))
        weight_grads.insert(0, mats_grad)
        small_grads.insert(0, small)
    stacked_w = tuple((jnp.stack([entry[slot] for entry in weight_grads]) for slot in range(4)))
    stacked_s = tuple((jnp.stack([entry[slot] for entry in small_grads]) for slot in range(5)))
    mp_index = lax.axis_index("mp")
    head_cols = qv_bias.shape[-1]
    up_cols = up_bias.shape[-1]
    grad_qv = lax.dynamic_slice_in_dim(stacked_s[3], mp_index * head_cols, head_cols, 2)
    grad_upb = lax.dynamic_slice_in_dim(stacked_s[4], mp_index * up_cols, up_cols, 1)
    return (
        state,
        gradient,
        stacked_w[0],
        grad_qv,
        stacked_w[1],
        stacked_w[2],
        grad_upb,
        stacked_w[3],
        stacked_s[0],
        stacked_s[1],
        stacked_s[2],
    )


def solution(mesh):
    placed = (
        P(("dp", "mp"), None),
        P(("dp", "mp"), None),
        P(),
        P(),
        P(),
        P(),
        P(None, "dp", None, "mp"),
        P(None, None, "mp"),
        P(None, ("mp", "dp"), None),
        P(None, "dp", "mp"),
        P(None, "mp"),
        P(None, ("mp", "dp"), None),
        P(),
    )
    return jax.shard_map(
        body,
        mesh=mesh,
        in_specs=placed,
        out_specs=(
            P(("dp", "mp"), None),
            P(("dp", "mp"), None),
            P(None, "dp", None, "mp"),
            P(None, None, "mp"),
            P(None, ("mp", "dp"), None),
            P(None, "dp", "mp"),
            P(None, "mp"),
            P(None, ("mp", "dp"), None),
            P(),
            P(),
            P(),
        ),
        check_vma=False,
    )
```

profile of v0, /device:TPU:0, one launch (start us, length us, event | category | flops | bytes accessed | tf_op | source)
XLA Modules:
  0.0 1947.3 jit_solution(16931985044161411071)
XLA Ops:
  14.8 39.2 %all-gather.39.cloned.1.call-done = bf16[1,768,3,384]{3,1,2,0:T(8,128)(2,1)} async-done(((bf16[1,48,3,384]{3,1,2,0:T(8,128)(2,1)}), bf16[1,768,3,384]{3,1,2,0:T(8,128)(2,1)}) %all-gather.39.cloned.1.call-update) | async-done | bytes 1769488 | tf_op jit(solution)/shard_map/all_gather | solution.py:84
  88.5 39.6 %all-gather.1 = bf16[1,384,768]{2,1,0:T(8,128)(2,1)} all-gather(bf16[1,24,768]{2,1,0:T(8,128)(2,1)S(1)} %get-tuple-element.207), channel_id=3, replica_groups=mesh['dp'=16,'mp'=2] {'dp'}, dimensions={1}, use_global_device_ids=true | all-gather | bytes 626688 | tf_op jit(solution)/shard_map/all_gather | solution.py:85
  198.3 32.1 %reduce-scatter.17.cloned.1.call-done = f32[384,768]{1,0:T(8,128)} async-done(((f32[768,768]{1,0:T(8,128)}), f32[384,768]{1,0:T(8,128)}) %reduce-scatter.17.cloned.1.call-update) | async-done | bytes 1179664 | tf_op jit(solution)/shard_map/reduce_scatter | solution.py:96
  235.6 39.8 %all-gather.41.cloned.1.call-done = bf16[1,768,1536]{2,1,0:T(8,128)(2,1)} async-done(((bf16[1,48,1536]{2,1,0:T(8,128)(2,1)}), bf16[1,768,1536]{2,1,0:T(8,128)(2,1)}) %all-gather.41.cloned.1.call-update) | async-done | bytes 2359312 | tf_op jit(solution)/shard_map/all_gather | solution.py:86
  275.4 23.5 %all-gather.25.cloned.1.call-done = bf16[768,768]{1,0:T(8,128)(2,1)} async-done(((bf16[384,768]{1,0:T(8,128)(2,1)}), bf16[768,768]{1,0:T(8,128)(2,1)}) %all-gather.25.cloned.1.call-update) | async-done | bytes 1179664 | tf_op jit(solution)/shard_map/all_gather | solution.py:92
  305.9 38.0 %all-gather.43.cloned.1.call-done = bf16[1,1536,768]{2,1,0:T(8,128)(2,1)} async-done(((bf16[1,96,768]{2,1,0:T(8,128)(2,1)}), bf16[1,1536,768]{2,1,0:T(8,128)(2,1)}) %all-gather.43.cloned.1.call-update) | async-done | bytes 2359312 | tf_op jit(solution)/shard_map/all_gather | solution.py:87
  350.5 32.9 %reduce-scatter.19.cloned.1.call-done = f32[384,768]{1,0:T(8,128)} async-done(((f32[768,768]{1,0:T(8,128)}), f32[384,768]{1,0:T(8,128)}) %reduce-scatter.19.cloned.1.call-update) | async-done | bytes 1179664 | tf_op jit(solution)/shard_map/reduce_scatter | solution.py:96
  387.1 39.1 %all-gather.45.cloned.1.call-done = bf16[1,768,3,384]{3,1,2,0:T(8,128)(2,1)} async-done(((bf16[1,48,3,384]{3,1,2,0:T(8,128)(2,1)}), bf16[1,768,3,384]{3,1,2,0:T(8,128)(2,1)}) %all-gather.45.cloned.1.call-update) | async-done | bytes 1769488 | tf_op jit(solution)/shard_map/all_gather | solution.py:84
  428.8 21.0 %all-gather.27.cloned.1.call-done = bf16[768,768]{1,0:T(8,128)(2,1)} async-done(((bf16[384,768]{1,0:T(8,128)(2,1)}), bf16[768,768]{1,0:T(8,128)(2,1)}) %all-gather.27.cloned.1.call-update) | async-done | bytes 1179664 | tf_op jit(solution)/shard_map/all_gather | solution.py:92
  457.2 39.2 %all-gather.5 = bf16[1,384,768]{2,1,0:T(8,128)(2,1)S(1)} all-gather(bf16[1,24,768]{2,1,0:T(8,128)(2,1)S(1)} %copy-done.50), channel_id=7, replica_groups=mesh['dp'=16,'mp'=2] {'dp'}, dimensions={1}, use_global_device_ids=true | all-gather | bytes 626688 | tf_op jit(solution)/shard_map/all_gather | solution.py:85
  557.9 33.6 %reduce-scatter.21.cloned.1.call-done = f32[384,768]{1,0:T(8,128)} async-done(((f32[768,768]{1,0:T(8,128)}), f32[384,768]{1,0:T(8,128)}) %reduce-scatter.21.cloned.1.call-update) | async-done | bytes 1179664 | tf_op jit(solution)/shard_map/reduce_scatter | solution.py:96
  599.2 37.5 %all-gather.47.cloned.1.call-done = bf16[1,768,1536]{2,1,0:T(8,128)(2,1)} async-done(((bf16[1,48,1536]{2,1,0:T(8,128)(2,1)}), bf16[1,768,1536]{2,1,0:T(8,128)(2,1)}) %all-gather.47.cloned.1.call-update) | async-done | bytes 2359312 | tf_op jit(solution)/shard_map/all_gather | solution.py:86
  636.7 23.5 %all-gather.29.cloned.1.call-done = bf16[768,768]{1,0:T(8,128)(2,1)} async-done(((bf16[384,768]{1,0:T(8,128)(2,1)}), bf16[768,768]{1,0:T(8,128)(2,1)}) %all-gather.29.cloned.1.call-update) | async-done | bytes 1179664 | tf_op jit(solution)/shard_map/all_gather | solution.py:92
  685.1 44.5 %all-gather.49.cloned.1.call-done = bf16[1,1536,768]{2,1,0:T(8,128)(2,1)} async-done(((bf16[1,96,768]{2,1,0:T(8,128)(2,1)}), bf16[1,1536,768]{2,1,0:T(8,128)(2,1)}) %all-gather.49.cloned.1.call-update) | async-done | bytes 2359312 | tf_op jit(solution)/shard_map/all_gather | solution.py:87
  746.7 27.8 %reduce-scatter.25.cloned.1.call-done = f32[384,768]{1,0:T(8,128)} async-done(((f32[768,768]{1,0:T(8,128)}), f32[384,768]{1,0:T(8,128)}) %reduce-scatter.25.cloned.1.call-update) | async-done | bytes 1179664 | tf_op jit(solution)/shard_map/reduce_scatter | solution.py:96
  777.9 33.6 %reduce-scatter.23.cloned.1.call-done = f32[384,768]{1,0:T(8,128)} async-done(((f32[768,768]{1,0:T(8,128)}), f32[384,768]{1,0:T(8,128)}) %reduce-scatter.23.cloned.1.call-update) | async-done | bytes 1179664 | tf_op jit(solution)/shard_map/reduce_scatter | solution.py:96
  818.3 22.4 %all-gather.33.cloned.1.call-done = bf16[768,768]{1,0:T(8,128)(2,1)} async-done(((bf16[384,768]{1,0:T(8,128)(2,1)}), bf16[768,768]{1,0:T(8,128)(2,1)}) %all-gather.33.cloned.1.call-update) | async-done | bytes 1179664 | tf_op jit(solution)/shard_map/all_gather | solution.py:92
  862.5 28.0 %multiply_convert_fusion.1 = bf16[6,768,2304]{2,1,0:T(8,128)(2,1)} fusion(f32[6,768,2304]{2,1,0:T(8,128)} %get-tuple-element.219, bf16[768,6,64]{0,2,1:T(8,128)(2,1)S(1)} %bitcast.283, f32[6,768]{1,0:T(8,128)S(1)} %bitcast.293, f32[6,768]{1,0:T(8,128)S(1)} %copy-done.74, pred[768,2304]{1,0:T(8,128)(4,1)S(1)} %fusion.7, ...), kind=kOutput, calls=%fused_computation.1 | convolution fusion | flops 1422655488 | bytes 67866624 | tf_op jit(solution)/shard_map/while/body/eval_jaxpr/qhd,khd->hqk/dot_general | solution.py:148
  941.3 41.2 %reduce-scatter.27.cloned.1.call-done = f32[384,768]{1,0:T(8,128)} async-done(((f32[768,768]{1,0:T(8,128)}), f32[384,768]{1,0:T(8,128)}) %reduce-scatter.27.cloned.1.call-update) | async-done | bytes 1179664 | tf_op jit(solution)/shard_map/reduce_scatter | solution.py:96
  988.1 22.9 %all-gather.35.cloned.1.call-done = bf16[768,768]{1,0:T(8,128)(2,1)} async-done(((bf16[384,768]{1,0:T(8,128)(2,1)}), bf16[768,768]{1,0:T(8,128)(2,1)}) %all-gather.35.cloned.1.call-update) | async-done | bytes 1179664 | tf_op jit(solution)/shard_map/all_gather | solution.py:92
  1022.2 34.9 %reduce-scatter.29.cloned.1.call-done = f32[384,768]{1,0:T(8,128)} async-done(((f32[768,768]{1,0:T(8,128)}), f32[384,768]{1,0:T(8,128)}) %reduce-scatter.29.cloned.1.call-update) | async-done | bytes 1179664 | tf_op jit(solution)/shard_map/reduce_scatter | solution.py:96
  1062.9 22.6 %all-gather.37.cloned.1.call-done = bf16[768,768]{1,0:T(8,128)(2,1)} async-done(((bf16[384,768]{1,0:T(8,128)(2,1)}), bf16[768,768]{1,0:T(8,128)(2,1)}) %all-gather.37.cloned.1.call-update) | async-done | bytes 1179664 | tf_op jit(solution)/shard_map/all_gather | solution.py:92
  1107.1 28.2 %multiply_convert_fusion = bf16[6,768,2304]{2,1,0:T(8,128)(2,1)} fusion(f32[6,768,2304]{2,1,0:T(8,128)} %get-tuple-element.215, bf16[768,6,64]{0,2,1:T(8,128)(2,1)S(1)} %bitcast.280, f32[6,768]{1,0:T(8,128)S(1)} %bitcast.292, f32[6,768]{1,0:T(8,128)S(1)} %copy-done.73, pred[768,2304]{1,0:T(8,128)(4,1)S(1)} %fusion.7, ...), kind=kOutput, calls=%fused_computation | convolution fusion | flops 1422655488 | bytes 67866624 | tf_op jit(solution)/shard_map/while/body/eval_jaxpr/qhd,khd->hqk/dot_general | solution.py:148
  1260.2 42.7 %reduce-scatter.47.cloned.1.call-done = f32[96,768]{1,0:T(8,128)} async-done(((f32[1536,768]{1,0:T(8,128)}), f32[96,768]{1,0:T(8,128)}) %reduce-scatter.47.cloned.1.call-update) | async-done | bytes 294928 | tf_op jit(solution)/shard_map/reduce_scatter | solution.py:340
  1302.9 78.5 %reduce-scatter.45.cloned.1.call-done = f32[96,768]{1,0:T(8,128)} async-done(((f32[1536,768]{1,0:T(8,128)}), f32[96,768]{1,0:T(8,128)}) %reduce-scatter.45.cloned.1.call-update) | async-done | bytes 294928 | tf_op jit(solution)/shard_map/reduce_scatter | solution.py:340
  1383.3 76.8 %reduce-scatter.43.cloned.1.call-done = f32[48,1536]{1,0:T(8,128)} async-done(((f32[768,1536]{1,0:T(8,128)}), f32[48,1536]{1,0:T(8,128)}) %reduce-scatter.43.cloned.1.call-update) | async-done | bytes 294928 | tf_op jit(solution)/shard_map/reduce_scatter | solution.py:339
  1460.1 78.5 %reduce-scatter.41.cloned.1.call-done = f32[48,1536]{1,0:T(8,128)} async-done(((f32[768,1536]{1,0:T(8,128)}), f32[48,1536]{1,0:T(8,128)}) %reduce-scatter.41.cloned.1.call-update) | async-done | bytes 294928 | tf_op jit(solution)/shard_map/reduce_scatter | solution.py:339
  1540.5 59.0 %reduce-scatter.39.cloned.1.call-done = f32[24,768]{1,0:T(8,128)} async-done(((f32[384,768]{1,0:T(8,128)}), f32[24,768]{1,0:T(8,128)}) %reduce-scatter.39.cloned.1.call-update) | async-done | bytes 73744 | tf_op jit(solution)/shard_map/reduce_scatter | solution.py:338
  1599.5 60.9 %reduce-scatter.37.cloned.1.call-done = f32[24,768]{1,0:T(8,128)} async-done(((f32[384,768]{1,0:T(8,128)}), f32[24,768]{1,0:T(8,128)}) %reduce-scatter.37.cloned.1.call-update) | async-done | bytes 73744 | tf_op jit(solution)/shard_map/reduce_scatter | solution.py:338
  1664.7 128.0 %all-reduce.3.cloned.1.call-done = (f32[1,2,768]{2,1,0:T(2,128)}, f32[1,2,768]{2,1,0:T(2,128)}, f32[1,3072]{1,0:T(1,128)}, f32[1,3072]{1,0:T(1,128)}, f32[1,2,76...) async-done(((f32[1,2,768]{2,1,0:T(2,128)}, f32[1,2,768]{2,1,0:T(2,128)}, ...) | async-done | bytes 73744 | tf_op jit(solution)/shard_map/psum | solution.py:342
  1799.2 68.4 %reduce-scatter.35.cloned.1.call-done = f32[48,3,384]{2,0,1:T(8,128)} async-done(((f32[768,3,384]{2,0,1:T(8,128)}), f32[48,3,384]{2,0,1:T(8,128)}) %reduce-scatter.35.cloned.1.call-update) | async-done | bytes 221200 | tf_op jit(solution)/shard_map/reduce_scatter | solution.py:337
  1867.6 70.9 %reduce-scatter.33.cloned.1.call-done = f32[48,3,384]{2,0,1:T(8,128)} async-done(((f32[768,3,384]{2,0,1:T(8,128)}), f32[48,3,384]{2,0,1:T(8,128)}) %reduce-scatter.33.cloned.1.call-update) | async-done | bytes 221200 | tf_op jit(solution)/shard_map/reduce_scatter | solution.py:337
  (444 shorter events, 523.2 us)
Async XLA Ops:
  9.0 68.7 %all-gather.23.cloned.1.call-start = ((), (), s32[]{:S(2)}) async-start(), calls=%async_computation.16 | async-start | bytes 1769472 | tf_op jit(solution)/shard_map/all_gather | solution.py:92
  13.4 217.0 %reduce-scatter.17.cloned.1.call-start = ((), (), s32[]{:S(2)}) async-start(), calls=%async_computation.17 | async-start | bytes 3538944 | tf_op jit(solution)/shard_map/reduce_scatter | solution.py:96
  82.9 49.3 %collective-permute-start.1 = (bf16[768,768]{0,1:T(8,128)(2,1)}, bf16[768,768]{0,1:T(8,128)(2,1)}, u32[]{:S(2)}, u32[]{:S(2)}) collective-permute-start(bf16[768,768]{0,1:T(8,128)(2,1)} %bitcast.6), channel_id=1, source_target_pairs={{2,0},{4,2},{6,4},{8,6},{10,8},{12,10},{14,12},{16,14},{18,16},{20... | collective-permute-start | bytes 3538952 | tf_op jit(solution)/shard_map/ppermute | solution.py:18
  84.2 48.0 %collective-permute-start = (bf16[768,768]{0,1:T(8,128)(2,1)}, bf16[768,768]{0,1:T(8,128)(2,1)}, u32[]{:S(2)}, u32[]{:S(2)}) collective-permute-start(bf16[768,768]{0,1:T(8,128)(2,1)} %bitcast.6), channel_id=1, source_target_pairs={{0,2},{2,4},{4,6},{6,8},{8,10},{10,12},{12,14},{14,16},{16,18},{18... | collective-permute-start | bytes 3538952 | tf_op jit(solution)/shard_map/ppermute | solution.py:15
  195.9 79.5 %all-gather.41.cloned.1.call-start = ((), (), s32[]{:S(2)}) async-start(), calls=%async_computation.41 | async-start | bytes 2506752 | tf_op jit(solution)/shard_map/all_gather | solution.py:86
  197.6 101.3 %all-gather.25.cloned.1.call-start = ((), (), s32[]{:S(2)}) async-start(), calls=%async_computation.18 | async-start | bytes 1769472 | tf_op jit(solution)/shard_map/all_gather | solution.py:92
  234.0 110.0 %all-gather.43.cloned.1.call-start = ((), (), s32[]{:S(2)}) async-start(), calls=%async_computation.42 | async-start | bytes 2506752 | tf_op jit(solution)/shard_map/all_gather | solution.py:87
  234.8 148.6 %reduce-scatter.19.cloned.1.call-start = ((), (), s32[]{:S(2)}) async-start(), calls=%async_computation.19 | async-start | bytes 3538944 | tf_op jit(solution)/shard_map/reduce_scatter | solution.py:96
  349.8 76.5 %all-gather.45.cloned.1.call-start = ((), (), s32[]{:S(2)}) async-start(), calls=%async_computation.43 | async-start | bytes 1880064 | tf_op jit(solution)/shard_map/all_gather | solution.py:84
  350.5 99.3 %all-gather.27.cloned.1.call-start = ((), (), s32[]{:S(2)}) async-start(), calls=%async_computation.20 | async-start | bytes 1769472 | tf_op jit(solution)/shard_map/all_gather | solution.py:92
  387.0 204.5 %reduce-scatter.21.cloned.1.call-start = ((), (), s32[]{:S(2)}) async-start(), calls=%async_computation.21 | async-start | bytes 3538944 | tf_op jit(solution)/shard_map/reduce_scatter | solution.py:96
  557.1 79.6 %all-gather.47.cloned.1.call-start = ((), (), s32[]{:S(2)}) async-start(), calls=%async_computation.44 | async-start | bytes 2506752 | tf_op jit(solution)/shard_map/all_gather | solution.py:86
  557.8 102.4 %all-gather.29.cloned.1.call-start = ((), (), s32[]{:S(2)}) async-start(), calls=%async_computation.22 | async-start | bytes 1769472 | tf_op jit(solution)/shard_map/all_gather | solution.py:92
  595.1 90.0 %all-gather.31.cloned.1.call-start = ((), (), s32[]{:S(2)}) async-start(), calls=%async_computation.24 | async-start | bytes 1769472 | tf_op jit(solution)/shard_map/all_gather | solution.py:92
  598.4 131.2 %all-gather.49.cloned.1.call-start = ((), (), s32[]{:S(2)}) async-start(), calls=%async_computation.45 | async-start | bytes 2506752 | tf_op jit(solution)/shard_map/all_gather | solution.py:87
  598.9 175.6 %reduce-scatter.25.cloned.1.call-start = ((), (), s32[]{:S(2)}) async-start(), calls=%async_computation.25 | async-start | bytes 3538944 | tf_op jit(solution)/shard_map/reduce_scatter | solution.py:96
  740.8 70.6 %reduce-scatter.23.cloned.1.call-start = ((), (), s32[]{:S(2)}) async-start(), calls=%async_computation.23 | async-start | bytes 3538944 | tf_op jit(solution)/shard_map/reduce_scatter | solution.py:96
  746.7 94.0 %all-gather.33.cloned.1.call-start = ((), (), s32[]{:S(2)}) async-start(), calls=%async_computation.26 | async-start | bytes 1769472 | tf_op jit(solution)/shard_map/all_gather | solution.py:92
  817.8 164.6 %reduce-scatter.27.cloned.1.call-start = ((), (), s32[]{:S(2)}) async-start(), calls=%async_computation.27 | async-start | bytes 3538944 | tf_op jit(solution)/shard_map/reduce_scatter | solution.py:96
  941.2 69.7 %all-gather.35.cloned.1.call-start = ((), (), s32[]{:S(2)}) async-start(), calls=%async_computation.28 | async-start | bytes 1769472 | tf_op jit(solution)/shard_map/all_gather | solution.py:92
  988.0 69.0 %reduce-scatter.29.cloned.1.call-start = ((), (), s32[]{:S(2)}) async-start(), calls=%async_computation.29 | async-start | bytes 3538944 | tf_op jit(solution)/shard_map/reduce_scatter | solution.py:96
  1022.2 63.4 %all-gather.37.cloned.1.call-start = ((), (), s32[]{:S(2)}) async-start(), calls=%async_computation.30 | async-start | bytes 1769472 | tf_op jit(solution)/shard_map/all_gather | solution.py:92
  1062.7 179.0 %reduce-scatter.31.cloned.1.call-start = ((), (), s32[]{:S(2)}) async-start(), calls=%async_computation.31 | async-start | bytes 3538944 | tf_op jit(solution)/shard_map/reduce_scatter | solution.py:96
  1182.4 120.5 %reduce-scatter.47.cloned.1.call-start = ((), (), s32[]{:S(2)}) async-start(), calls=%async_computation.39 | async-start | bytes 5013504 | tf_op jit(solution)/shard_map/reduce_scatter | solution.py:340
  1189.5 191.9 %reduce-scatter.45.cloned.1.call-start = ((), (), s32[]{:S(2)}) async-start(), calls=%async_computation.38 | async-start | bytes 5013504 | tf_op jit(solution)/shard_map/reduce_scatter | solution.py:340
  1196.7 263.4 %reduce-scatter.43.cloned.1.call-start = ((), (), s32[]{:S(2)}) async-start(), calls=%async_computation.37 | async-start | bytes 5013504 | tf_op jit(solution)/shard_map/reduce_scatter | solution.py:339
  1203.9 334.7 %reduce-scatter.41.cloned.1.call-start = ((), (), s32[]{:S(2)}) async-start(), calls=%async_computation.36 | async-start | bytes 5013504 | tf_op jit(solution)/shard_map/reduce_scatter | solution.py:339
  1211.0 388.5 %reduce-scatter.39.cloned.1.call-start = ((), (), s32[]{:S(2)}) async-start(), calls=%async_computation.35 | async-start | bytes 1253376 | tf_op jit(solution)/shard_map/reduce_scatter | solution.py:338
  1214.1 446.2 %reduce-scatter.37.cloned.1.call-start = ((), (), s32[]{:S(2)}) async-start(), calls=%async_computation.34 | async-start | bytes 1253376 | tf_op jit(solution)/shard_map/reduce_scatter | solution.py:338
  1217.8 574.8 %all-reduce.3.cloned.1.call-start = ((), (), s32[]{:S(2)}) async-start(), calls=%async_computation.46 | async-start | bytes 147456 | tf_op jit(solution)/shard_map/psum | solution.py:342
  1246.0 621.6 %reduce-scatter.35.cloned.1.call-start = ((), (), s32[]{:S(2)}) async-start(), calls=%async_computation.33 | async-start | bytes 3760128 | tf_op jit(solution)/shard_map/reduce_scatter | solution.py:337
  1251.0 687.5 %reduce-scatter.33.cloned.1.call-start = ((), (), s32[]{:S(2)}) async-start(), calls=%async_computation.32 | async-start | bytes 3760128 | tf_op jit(solution)/shard_map/reduce_scatter | solution.py:337
  (104 other events, 3123.2 us)
Sparse Core Ops, SparseCore 0:
  10.9 43.1 all-gather.38
  56.2 21.4 all-gather.22
  196.0 34.2 reduce-scatter.16
  233.1 42.2 all-gather.40
  277.4 21.4 all-gather.24
  301.6 42.2 all-gather.42
  349.9 33.5 reduce-scatter.18
  385.7 40.4 all-gather.44
  428.3 21.4 all-gather.26
  557.2 34.2 reduce-scatter.20
  594.4 42.2 all-gather.46
  638.7 21.4 all-gather.28
  662.3 22.7 all-gather.30
  687.2 42.2 all-gather.48
  741.0 33.5 reduce-scatter.24
  776.6 34.7 reduce-scatter.22
  817.9 22.7 all-gather.32
  941.4 41.0 reduce-scatter.26
  988.2 22.7 all-gather.34
  1022.3 34.7 reduce-scatter.28
  1062.8 22.7 all-gather.36
  1182.5 40.8 reduce-scatter.30
  1227.3 75.5 reduce-scatter.46
  1306.6 74.7 reduce-scatter.44
  1385.3 74.7 reduce-scatter.42
  1463.8 74.7 reduce-scatter.40
  1542.1 57.3 reduce-scatter.38
  1603.1 57.1 reduce-scatter.36
  1667.9 124.6 all-reduce.2
  1796.3 71.2 reduce-scatter.34
  1871.5 66.9 reduce-scatter.32
where the time goes:
time: 1950 us
  waiting for transfers between devices  1310 us (67%)
  matrix products  312 us (16%)
  other arithmetic  129 us (7%)
  blocking collectives  78.8 us (4%)
  local copies, waits for them, and re-layouts  73.5 us (4%)
  starting transfers between devices  23.5 us (1%)
    reduce_scatter x8, waiting for transfers between devices, sum_rows(): lax.psum_scatter(jnp.dot(left, right, preferred_element_type=jnp.float32)...  236 us
    all_gather x8, waiting for transfers between devices, gather_rows(): return lax.all_gather(values, 'mp', axis=0, tiled=True)  175 us
    reduce_scatter x2, waiting for transfers between devices, body(): lax.psum_scatter(mats_grad[2], 'dp', scatter_dimension=0, tiled=True)  155 us
    reduce_scatter x2, waiting for transfers between devices, body(): lax.psum_scatter(mats_grad[0], 'dp', scatter_dimension=0, tiled=True)  139 us
    psum x1, waiting for transfers between devices, body(): lax.psum((small[0], small[1], small[2], small[3], small[4]), ('dp', 'mp'))  128 us
    reduce_scatter x2, waiting for transfers between devices, body(): lax.psum_scatter(mats_grad[3], 'dp', scatter_dimension=0, tiled=True)  121 us
    reduce_scatter x2, waiting for transfers between devices, body(): lax.psum_scatter(mats_grad[1], 'dp', scatter_dimension=0, tiled=True)  120 us
    all_gather x2, waiting for transfers between devices, fetch_weights(): lax.all_gather(down_weight[depth], 'dp', axis=0, tiled=True)  82.5 us
  transfers between devices with their start and end apart: 39, of which 30 were waited for; matrix products, arithmetic and copies ran while one was open for 9% of the time, Pallas kernels for 0%

commit v1 on v0

--- a/solution.py
+++ b/solution.py
@@ -1,3 +1,4 @@
+import functools
 import jax
 import jax.numpy as jnp
 from jax import lax
@@ -5,6 +6,29 @@
 
 HD = 64
 epsilon = 1e-05
+
+
+def _play_stages_all(frame, comm_axis):
+    s_next, clean, plain = (
+        jax.lax.psum(1, comm_axis),
+        jax.lax.axis_index(comm_axis),
+        frame.shape[0],
+    )
+    value_now = map(lambda ix: (ix, (ix + 1) % s_next), range(s_next))
+    history = list(value_now)
+    later = jnp.zeros((*frame.shape[:0], s_next * plain, *frame.shape[1:]), frame.dtype)
+    val2 = frame
+    m = 0
+    while m < s_next:
+        v_next = (clean - m) % s_next
+        later = lax.dynamic_update_slice_in_dim(later, val2, v_next * plain, axis=0)
+        if m < s_next - 1:
+            val2 = jax.lax.ppermute(val2, comm_axis, perm=history)
+        m = m + 1
+    return later
+
+
+feed_object = functools.partial(_play_stages_all, comm_axis="dp")
 
 
 def padded_2(block, sides, width):
@@ -83,7 +107,7 @@
     return (
         lax.all_gather(qkv_weight[depth], "dp", axis=0, tiled=True),
         lax.all_gather(proj_weight[depth], "dp", axis=0, tiled=True),
-        lax.all_gather(up_weight[depth], "dp", axis=0, tiled=True),
+        feed_object(up_weight[depth]),
         lax.all_gather(down_weight[depth], "dp", axis=0, tiled=True),
     )
 

time: 1950 us -> 1960 us (level)
  local copies, waits for them, and re-layouts: 73.5 us -> 107 us
  waiting for transfers between devices: 1310 us -> 1290 us
    ppermute x0 -> x30, waiting for transfers between devices: none -> 200 us  [_play_stages_all(): val2 = jax.lax.ppermute(val2, comm_axis, perm=history)]
    all_gather x2, waiting for transfers between devices: 82.5 us -> 0.01 us  [fetch_weights(): lax.all_gather(down_weight[depth], 'dp', axis=0, tiled=True)]
    all_gather x2 -> x0, waiting for transfers between devices: 77.2 us -> none  [fetch_weights(): lax.all_gather(up_weight[depth], 'dp', axis=0, tiled=True)]
    all_gather x8, waiting for transfers between devices: 175 us -> 110 us  [gather_rows(): return lax.all_gather(values, 'mp', axis=0, tiled=True)]
    dynamic_update_slice x0 -> x32, local copies, waits for them, and re-layouts: none -> 22.4 us  [_play_stages_all(): later = lax.dynamic_update_slice_in_dim(later, val2, v_next * plain, axis=0)]
  transfers between devices with their start and end apart: 39 -> 67, of which waited for: 30 -> 53; matrix products, arithmetic and copies ran while one was open for 9% -> 10% of each run, Pallas kernels for 0% -> 0%
where the time goes in v1:
time: 1960 us; the launch traced here: 1950 us
  waiting for transfers between devices  1290 us (66%)
  matrix products  311 us (16%)
  other arithmetic  125 us (6%)
  local copies, waits for them, and re-layouts  107 us (5%)
  blocking collectives  80.2 us (4%)
  starting transfers between devices  23.6 us (1%)
    reduce_scatter x8, waiting for transfers between devices, sum_rows(): lax.psum_scatter(jnp.dot(left, right, preferred_element_type=jnp.float32)...  234 us
    ppermute x30, waiting for transfers between devices, _play_stages_all(): val2 = jax.lax.ppermute(val2, comm_axis, perm=history)  200 us
    reduce_scatter x2, waiting for transfers between devices, body(): lax.psum_scatter(mats_grad[2], 'dp', scatter_dimension=0, tiled=True)  155 us
    reduce_scatter x2, waiting for transfers between devices, body(): lax.psum_scatter(mats_grad[0], 'dp', scatter_dimension=0, tiled=True)  139 us
    psum x1, waiting for transfers between devices, body(): lax.psum((small[0], small[1], small[2], small[3], small[4]), ('dp', 'mp'))  128 us
    reduce_scatter x2, waiting for transfers between devices, body(): lax.psum_scatter(mats_grad[3], 'dp', scatter_dimension=0, tiled=True)  123 us
    reduce_scatter x2, waiting for transfers between devices, body(): lax.psum_scatter(mats_grad[1], 'dp', scatter_dimension=0, tiled=True)  120 us
    all_gather x8, waiting for transfers between devices, gather_rows(): return lax.all_gather(values, 'mp', axis=0, tiled=True)  110 us
  transfers between devices with their start and end apart: 67, of which 53 were waited for; matrix products, arithmetic and copies ran while one was open for 10% of the time, Pallas kernels for 0%

profile of v1, /device:TPU:0, one launch (start us, length us, event | category | flops | bytes accessed | tf_op | source)
XLA Modules:
  0.0 1953.2 jit_solution(7616251466650162325)
XLA Ops:
  15.6 38.5 %all-gather.35.cloned.1.call-done = bf16[1,768,3,384]{3,1,2,0:T(8,128)(2,1)} async-done(((bf16[1,48,3,384]{3,1,2,0:T(8,128)(2,1)}), bf16[1,768,3,384]{3,1,2,0:T(8,128)(2,1)}) %all-gather.35.cloned.1.call-update) | async-done | bytes 1769488 | tf_op jit(solution)/shard_map/all_gather | solution.py:108
  56.7 21.0 %all-gather.19.cloned.1.call-done = bf16[768,768]{1,0:T(8,128)(2,1)} async-done(((bf16[384,768]{1,0:T(8,128)(2,1)}), bf16[768,768]{1,0:T(8,128)(2,1)}) %all-gather.19.cloned.1.call-update) | async-done | bytes 1179664 | tf_op jit(solution)/shard_map/all_gather | solution.py:116
  88.5 39.6 %all-gather.1 = bf16[1,384,768]{2,1,0:T(8,128)(2,1)} all-gather(bf16[1,24,768]{2,1,0:T(8,128)(2,1)S(1)} %get-tuple-element.207), channel_id=3, replica_groups=mesh['dp'=16,'mp'=2] {'dp'}, dimensions={1}, use_global_device_ids=true | all-gather | bytes 626688 | tf_op jit(solution)/shard_map/all_gather | solution.py:109
  153.9 20.7 %exponential_reduce_fusion.1 = f32[6,768]{1,0:T(8,128)S(1)} fusion(f32[6,768,2304]{2,1,0:T(8,128)} %get-tuple-element.215, f32[6,768]{1,0:T(8,128)} %get-tuple-element.214, pred[768,2304]{1,0:T(8,128)(4,1)S(1)} %fusion.7), kind=kLoop, calls=%fused_computation.6 | loop fusion | flops 42462720 | bytes 44273664 | tf_op jit(solution)/shard_map/while/body/eval_jaxpr/reduce_sum | solution.py:148
  197.5 33.0 %reduce-scatter.17.cloned.1.call-done = f32[384,768]{1,0:T(8,128)} async-done(((f32[768,768]{1,0:T(8,128)}), f32[384,768]{1,0:T(8,128)}) %reduce-scatter.17.cloned.1.call-update) | async-done | bytes 1179664 | tf_op jit(solution)/shard_map/reduce_scatter | solution.py:120
  362.7 31.1 %reduce-scatter.19.cloned.1.call-done = f32[384,768]{1,0:T(8,128)} async-done(((f32[768,768]{1,0:T(8,128)}), f32[384,768]{1,0:T(8,128)}) %reduce-scatter.19.cloned.1.call-update) | async-done | bytes 1179664 | tf_op jit(solution)/shard_map/reduce_scatter | solution.py:120
  397.5 39.1 %all-gather.39.cloned.1.call-done = bf16[1,768,3,384]{3,1,2,0:T(8,128)(2,1)} async-done(((bf16[1,48,3,384]{3,1,2,0:T(8,128)(2,1)}), bf16[1,768,3,384]{3,1,2,0:T(8,128)(2,1)}) %all-gather.39.cloned.1.call-update) | async-done | bytes 1769488 | tf_op jit(solution)/shard_map/all_gather | solution.py:108
  439.2 21.0 %all-gather.23.cloned.1.call-done = bf16[768,768]{1,0:T(8,128)(2,1)} async-done(((bf16[384,768]{1,0:T(8,128)(2,1)}), bf16[768,768]{1,0:T(8,128)(2,1)}) %all-gather.23.cloned.1.call-update) | async-done | bytes 1179664 | tf_op jit(solution)/shard_map/all_gather | solution.py:116
  467.6 40.6 %all-gather.4 = bf16[1,384,768]{2,1,0:T(8,128)(2,1)} all-gather(bf16[1,24,768]{2,1,0:T(8,128)(2,1)S(1)} %copy-done.56), channel_id=6, replica_groups=mesh['dp'=16,'mp'=2] {'dp'}, dimensions={1}, use_global_device_ids=true | all-gather | bytes 626688 | tf_op jit(solution)/shard_map/all_gather | solution.py:109
  527.8 19.9 %exponential_reduce_fusion = f32[6,768]{1,0:T(8,128)S(1)} fusion(f32[6,768,2304]{2,1,0:T(8,128)} %get-tuple-element.219, f32[6,768]{1,0:T(8,128)S(1)} %get-tuple-element.218, pred[768,2304]{1,0:T(8,128)(4,1)S(1)} %fusion.7), kind=kLoop, calls=%fused_computation.3 | loop fusion | flops 42462720 | bytes 44273664 | tf_op jit(solution)/shard_map/while/body/eval_jaxpr/reduce_sum | solution.py:148
  547.7 18.2 fusion.50
  569.5 34.4 %reduce-scatter.21.cloned.1.call-done = f32[384,768]{1,0:T(8,128)} async-done(((f32[768,768]{1,0:T(8,128)}), f32[384,768]{1,0:T(8,128)}) %reduce-scatter.21.cloned.1.call-update) | async-done | bytes 1179664 | tf_op jit(solution)/shard_map/reduce_scatter | solution.py:120
  750.8 26.2 %reduce-scatter.25.cloned.1.call-done = f32[384,768]{1,0:T(8,128)} async-done(((f32[768,768]{1,0:T(8,128)}), f32[384,768]{1,0:T(8,128)}) %reduce-scatter.25.cloned.1.call-update) | async-done | bytes 1179664 | tf_op jit(solution)/shard_map/reduce_scatter | solution.py:120
  780.3 33.6 %reduce-scatter.23.cloned.1.call-done = f32[384,768]{1,0:T(8,128)} async-done(((f32[768,768]{1,0:T(8,128)}), f32[384,768]{1,0:T(8,128)}) %reduce-scatter.23.cloned.1.call-update) | async-done | bytes 1179664 | tf_op jit(solution)/shard_map/reduce_scatter | solution.py:120
  820.6 22.7 %all-gather.29.cloned.1.call-done = bf16[768,768]{1,0:T(8,128)(2,1)} async-done(((bf16[384,768]{1,0:T(8,128)(2,1)}), bf16[768,768]{1,0:T(8,128)(2,1)}) %all-gather.29.cloned.1.call-update) | async-done | bytes 1179664 | tf_op jit(solution)/shard_map/all_gather | solution.py:116
  845.6 19.4 convolution_bitcast_fusion.1
  865.0 28.1 %multiply_convert_fusion.1 = bf16[6,768,2304]{2,1,0:T(8,128)(2,1)} fusion(f32[6,768,2304]{2,1,0:T(8,128)} %get-tuple-element.219, bf16[768,6,64]{0,2,1:T(8,128)(2,1)S(1)} %bitcast.281, f32[6,768]{1,0:T(8,128)S(1)} %bitcast.291, f32[6,768]{1,0:T(8,128)S(1)} %copy-done.82, pred[768,2304]{1,0:T(8,128)(4,1)S(1)} %fusion.7, ...), kind=kOutput, calls=%fused_computation.1 | convolution fusion | flops 1422655488 | bytes 67866624 | tf_op jit(solution)/shard_map/while/body/eval_jaxpr/qhd,khd->hqk/dot_general | solution.py:172
  944.1 40.9 %reduce-scatter.27.cloned.1.call-done = f32[384,768]{1,0:T(8,128)} async-done(((f32[768,768]{1,0:T(8,128)}), f32[384,768]{1,0:T(8,128)}) %reduce-scatter.27.cloned.1.call-update) | async-done | bytes 1179664 | tf_op jit(solution)/shard_map/reduce_scatter | solution.py:120
  990.7 22.9 %all-gather.31.cloned.1.call-done = bf16[768,768]{1,0:T(8,128)(2,1)} async-done(((bf16[384,768]{1,0:T(8,128)(2,1)}), bf16[768,768]{1,0:T(8,128)(2,1)}) %all-gather.31.cloned.1.call-update) | async-done | bytes 1179664 | tf_op jit(solution)/shard_map/all_gather | solution.py:116
  1026.3 34.9 %reduce-scatter.29.cloned.1.call-done = f32[384,768]{1,0:T(8,128)} async-done(((f32[768,768]{1,0:T(8,128)}), f32[384,768]{1,0:T(8,128)}) %reduce-scatter.29.cloned.1.call-update) | async-done | bytes 1179664 | tf_op jit(solution)/shard_map/reduce_scatter | solution.py:120
  1067.0 22.7 %all-gather.33.cloned.1.call-done = bf16[768,768]{1,0:T(8,128)(2,1)} async-done(((bf16[384,768]{1,0:T(8,128)(2,1)}), bf16[768,768]{1,0:T(8,128)(2,1)}) %all-gather.33.cloned.1.call-update) | async-done | bytes 1179664 | tf_op jit(solution)/shard_map/all_gather | solution.py:116
  1091.8 19.4 convolution_bitcast_fusion
  1111.2 28.1 %multiply_convert_fusion = bf16[6,768,2304]{2,1,0:T(8,128)(2,1)} fusion(f32[6,768,2304]{2,1,0:T(8,128)} %get-tuple-element.215, bf16[768,6,64]{0,2,1:T(8,128)(2,1)S(1)} %bitcast.278, f32[6,768]{1,0:T(8,128)S(1)} %bitcast.290, f32[6,768]{1,0:T(8,128)S(1)} %copy-done.80, pred[768,2304]{1,0:T(8,128)(4,1)S(1)} %fusion.7, ...), kind=kOutput, calls=%fused_computation | convolution fusion | flops 1422655488 | bytes 67866624 | tf_op jit(solution)/shard_map/while/body/eval_jaxpr/qhd,khd->hqk/dot_general | solution.py:172
  1264.5 44.5 %reduce-scatter.47.cloned.1.call-done = f32[96,768]{1,0:T(8,128)} async-done(((f32[1536,768]{1,0:T(8,128)}), f32[96,768]{1,0:T(8,128)}) %reduce-scatter.47.cloned.1.call-update) | async-done | bytes 294928 | tf_op jit(solution)/shard_map/reduce_scatter | solution.py:364
  1309.0 78.6 %reduce-scatter.45.cloned.1.call-done = f32[96,768]{1,0:T(8,128)} async-done(((f32[1536,768]{1,0:T(8,128)}), f32[96,768]{1,0:T(8,128)}) %reduce-scatter.45.cloned.1.call-update) | async-done | bytes 294928 | tf_op jit(solution)/shard_map/reduce_scatter | solution.py:364
  1389.5 76.8 %reduce-scatter.43.cloned.1.call-done = f32[48,1536]{1,0:T(8,128)} async-done(((f32[768,1536]{1,0:T(8,128)}), f32[48,1536]{1,0:T(8,128)}) %reduce-scatter.43.cloned.1.call-update) | async-done | bytes 294928 | tf_op jit(solution)/shard_map/reduce_scatter | solution.py:363
  1466.3 78.5 %reduce-scatter.41.cloned.1.call-done = f32[48,1536]{1,0:T(8,128)} async-done(((f32[768,1536]{1,0:T(8,128)}), f32[48,1536]{1,0:T(8,128)}) %reduce-scatter.41.cloned.1.call-update) | async-done | bytes 294928 | tf_op jit(solution)/shard_map/reduce_scatter | solution.py:363
  1546.7 59.1 %reduce-scatter.39.cloned.1.call-done = f32[24,768]{1,0:T(8,128)} async-done(((f32[384,768]{1,0:T(8,128)}), f32[24,768]{1,0:T(8,128)}) %reduce-scatter.39.cloned.1.call-update) | async-done | bytes 73744 | tf_op jit(solution)/shard_map/reduce_scatter | solution.py:362
  1605.8 60.7 %reduce-scatter.37.cloned.1.call-done = f32[24,768]{1,0:T(8,128)} async-done(((f32[384,768]{1,0:T(8,128)}), f32[24,768]{1,0:T(8,128)}) %reduce-scatter.37.cloned.1.call-update) | async-done | bytes 73744 | tf_op jit(solution)/shard_map/reduce_scatter | solution.py:362
  1670.2 128.3 %all-reduce.3.cloned.1.call-done = (f32[1,2,768]{2,1,0:T(2,128)}, f32[1,2,768]{2,1,0:T(2,128)}, f32[1,3072]{1,0:T(1,128)}, f32[1,3072]{1,0:T(1,128)}, f32[1,2,76...) async-done(((f32[1,2,768]{2,1,0:T(2,128)}, f32[1,2,768]{2,1,0:T(2,128)}, ...) | async-done | bytes 73744 | tf_op jit(solution)/shard_map/psum | solution.py:366
  1805.2 68.5 %reduce-scatter.35.cloned.1.call-done = f32[48,3,384]{2,0,1:T(8,128)} async-done(((f32[768,3,384]{2,0,1:T(8,128)}), f32[48,3,384]{2,0,1:T(8,128)}) %reduce-scatter.35.cloned.1.call-update) | async-done | bytes 221200 | tf_op jit(solution)/shard_map/reduce_scatter | solution.py:361
  1873.7 70.9 %reduce-scatter.33.cloned.1.call-done = f32[48,3,384]{2,0,1:T(8,128)} async-done(((f32[768,3,384]{2,0,1:T(8,128)}), f32[48,3,384]{2,0,1:T(8,128)}) %reduce-scatter.33.cloned.1.call-update) | async-done | bytes 221200 | tf_op jit(solution)/shard_map/reduce_scatter | solution.py:361
  (544 shorter events, 616.0 us)
Async XLA Ops:
  7.2 46.9 %all-gather.35.cloned.1.call-start = ((), (), s32[]{:S(2)}) async-start(), calls=%async_computation.40 | async-start | bytes 1880064 | tf_op jit(solution)/shard_map/all_gather | solution.py:108
  9.0 68.6 %all-gather.19.cloned.1.call-start = ((), (), s32[]{:S(2)}) async-start(), calls=%async_computation.16 | async-start | bytes 1769472 | tf_op jit(solution)/shard_map/all_gather | solution.py:116
  14.1 216.3 %reduce-scatter.17.cloned.1.call-start = ((), (), s32[]{:S(2)}) async-start(), calls=%async_computation.17 | async-start | bytes 3538944 | tf_op jit(solution)/shard_map/reduce_scatter | solution.py:120
  82.9 49.3 %collective-permute-start.1 = (bf16[768,768]{0,1:T(8,128)(2,1)}, bf16[768,768]{0,1:T(8,128)(2,1)}, u32[]{:S(2)}, u32[]{:S(2)}) collective-permute-start(bf16[768,768]{0,1:T(8,128)(2,1)} %bitcast.6), channel_id=1, source_target_pairs={{2,0},{4,2},{6,4},{8,6},{10,8},{12,10},{14,12},{16,14},{18,16},{20... | collective-permute-start | bytes 3538952 | tf_op jit(solution)/shard_map/ppermute | solution.py:42
  84.2 48.0 %collective-permute-start = (bf16[768,768]{0,1:T(8,128)(2,1)}, bf16[768,768]{0,1:T(8,128)(2,1)}, u32[]{:S(2)}, u32[]{:S(2)}) collective-permute-start(bf16[768,768]{0,1:T(8,128)(2,1)} %bitcast.6), channel_id=1, source_target_pairs={{0,2},{2,4},{4,6},{6,8},{8,10},{10,12},{12,14},{14,16},{16,18},{18... | collective-permute-start | bytes 3538952 | tf_op jit(solution)/shard_map/ppermute | solution.py:39
  196.0 153.1 %all-gather.21.cloned.1.call-start = ((), (), s32[]{:S(2)}) async-start(), calls=%async_computation.18 | async-start | bytes 1769472 | tf_op jit(solution)/shard_map/all_gather | solution.py:116
  234.1 122.1 %all-gather.37.cloned.1.call-start = ((), (), s32[]{:S(2)}) async-start(), calls=%async_computation.41 | async-start | bytes 2506752 | tf_op jit(solution)/shard_map/all_gather | solution.py:111
  235.6 158.2 %reduce-scatter.19.cloned.1.call-start = ((), (), s32[]{:S(2)}) async-start(), calls=%async_computation.19 | async-start | bytes 3538944 | tf_op jit(solution)/shard_map/reduce_scatter | solution.py:120
  361.9 74.7 %all-gather.39.cloned.1.call-start = ((), (), s32[]{:S(2)}) async-start(), calls=%async_computation.42 | async-start | bytes 1880064 | tf_op jit(solution)/shard_map/all_gather | solution.py:108
  362.7 97.5 %all-gather.23.cloned.1.call-start = ((), (), s32[]{:S(2)}) async-start(), calls=%async_computation.20 | async-start | bytes 1769472 | tf_op jit(solution)/shard_map/all_gather | solution.py:116
  397.4 206.5 %reduce-scatter.21.cloned.1.call-start = ((), (), s32[]{:S(2)}) async-start(), calls=%async_computation.21 | async-start | bytes 3538944 | tf_op jit(solution)/shard_map/reduce_scatter | solution.py:120
  463.1 45.1 %collective-permute-start.18 = (bf16[768,768]{0,1:T(8,128)(2,1)S(1)}, bf16[768,768]{0,1:T(8,128)(2,1)S(1)}, u32[]{:S(2)}, u32[]{:S(2)}) collective-permute-start(bf16[768,768]{0,1:T(8,128)(2,1)S(1)} %bitcast.265), channel_id=1, source_target_pairs={{2,0},{4,2},{6,4},{8,6},{10,8},{12,10},{14,12},{16,14},{18,16},{20... | collective-permute-start | bytes 3538952 | tf_op jit(solution)/shard_map/ppermute | solution.py:42
  569.4 155.7 %all-gather.25.cloned.1.call-start = ((), (), s32[]{:S(2)}) async-start(), calls=%async_computation.22 | async-start | bytes 1769472 | tf_op jit(solution)/shard_map/all_gather | solution.py:116
  607.5 124.6 %all-gather.27.cloned.1.call-start = ((), (), s32[]{:S(2)}) async-start(), calls=%async_computation.24 | async-start | bytes 1769472 | tf_op jit(solution)/shard_map/all_gather | solution.py:116
  610.8 121.3 %all-gather.41.cloned.1.call-start = ((), (), s32[]{:S(2)}) async-start(), calls=%async_computation.43 | async-start | bytes 2506752 | tf_op jit(solution)/shard_map/all_gather | solution.py:111
  611.4 165.6 %reduce-scatter.25.cloned.1.call-start = ((), (), s32[]{:S(2)}) async-start(), calls=%async_computation.25 | async-start | bytes 3538944 | tf_op jit(solution)/shard_map/reduce_scatter | solution.py:120
  744.9 69.0 %reduce-scatter.23.cloned.1.call-start = ((), (), s32[]{:S(2)}) async-start(), calls=%async_computation.23 | async-start | bytes 3538944 | tf_op jit(solution)/shard_map/reduce_scatter | solution.py:120
  750.8 92.5 %all-gather.29.cloned.1.call-start = ((), (), s32[]{:S(2)}) async-start(), calls=%async_computation.26 | async-start | bytes 1769472 | tf_op jit(solution)/shard_map/all_gather | solution.py:116
  820.3 164.7 %reduce-scatter.27.cloned.1.call-start = ((), (), s32[]{:S(2)}) async-start(), calls=%async_computation.27 | async-start | bytes 3538944 | tf_op jit(solution)/shard_map/reduce_scatter | solution.py:120
  944.1 69.4 %all-gather.31.cloned.1.call-start = ((), (), s32[]{:S(2)}) async-start(), calls=%async_computation.28 | async-start | bytes 1769472 | tf_op jit(solution)/shard_map/all_gather | solution.py:116
  990.6 70.6 %reduce-scatter.29.cloned.1.call-start = ((), (), s32[]{:S(2)}) async-start(), calls=%async_computation.29 | async-start | bytes 3538944 | tf_op jit(solution)/shard_map/reduce_scatter | solution.py:120
  1026.3 63.4 %all-gather.33.cloned.1.call-start = ((), (), s32[]{:S(2)}) async-start(), calls=%async_computation.30 | async-start | bytes 1769472 | tf_op jit(solution)/shard_map/all_gather | solution.py:116
  1066.7 178.8 %reduce-scatter.31.cloned.1.call-start = ((), (), s32[]{:S(2)}) async-start(), calls=%async_computation.31 | async-start | bytes 3538944 | tf_op jit(solution)/shard_map/reduce_scatter | solution.py:120
  1189.4 119.6 %reduce-scatter.47.cloned.1.call-start = ((), (), s32[]{:S(2)}) async-start(), calls=%async_computation.39 | async-start | bytes 5013504 | tf_op jit(solution)/shard_map/reduce_scatter | solution.py:364
  1194.9 192.7 %reduce-scatter.45.cloned.1.call-start = ((), (), s32[]{:S(2)}) async-start(), calls=%async_computation.38 | async-start | bytes 5013504 | tf_op jit(solution)/shard_map/reduce_scatter | solution.py:364
  1201.3 265.0 %reduce-scatter.43.cloned.1.call-start = ((), (), s32[]{:S(2)}) async-start(), calls=%async_computation.37 | async-start | bytes 5013504 | tf_op jit(solution)/shard_map/reduce_scatter | solution.py:363
  1207.6 337.2 %reduce-scatter.41.cloned.1.call-start = ((), (), s32[]{:S(2)}) async-start(), calls=%async_computation.36 | async-start | bytes 5013504 | tf_op jit(solution)/shard_map/reduce_scatter | solution.py:363
  1213.7 392.1 %reduce-scatter.39.cloned.1.call-start = ((), (), s32[]{:S(2)}) async-start(), calls=%async_computation.35 | async-start | bytes 1253376 | tf_op jit(solution)/shard_map/reduce_scatter | solution.py:362
  1216.9 449.6 %reduce-scatter.37.cloned.1.call-start = ((), (), s32[]{:S(2)}) async-start(), calls=%async_computation.34 | async-start | bytes 1253376 | tf_op jit(solution)/shard_map/reduce_scatter | solution.py:362
  1221.8 576.8 %all-reduce.3.cloned.1.call-start = ((), (), s32[]{:S(2)}) async-start(), calls=%async_computation.44 | async-start | bytes 147456 | tf_op jit(solution)/shard_map/psum | solution.py:366
  1249.3 624.4 %reduce-scatter.35.cloned.1.call-start = ((), (), s32[]{:S(2)}) async-start(), calls=%async_computation.33 | async-start | bytes 3760128 | tf_op jit(solution)/shard_map/reduce_scatter | solution.py:361
  1254.3 690.3 %reduce-scatter.33.cloned.1.call-start = ((), (), s32[]{:S(2)}) async-start(), calls=%async_computation.32 | async-start | bytes 3760128 | tf_op jit(solution)/shard_map/reduce_scatter | solution.py:361
  (138 other events, 3220.3 us)
Sparse Core Ops, SparseCore 0:
  10.9 43.1 all-gather.34
  56.2 21.4 all-gather.18
  196.1 34.2 reduce-scatter.16
  234.2 22.7 all-gather.20
  259.7 44.0 all-gather.36
  362.0 31.7 reduce-scatter.18
  396.1 40.4 all-gather.38
  438.7 21.4 all-gather.22
  569.6 34.2 reduce-scatter.20
  607.6 22.7 all-gather.24
  631.9 22.7 all-gather.26
  657.4 43.7 all-gather.40
  745.0 31.9 reduce-scatter.24
  779.1 34.7 reduce-scatter.22
  820.4 22.7 all-gather.28
  944.2 40.7 reduce-scatter.26
  990.7 22.7 all-gather.30
  1026.4 34.7 reduce-scatter.28
  1066.9 22.7 all-gather.32
  1189.6 39.9 reduce-scatter.30
  1233.4 75.5 reduce-scatter.46
  1312.9 74.6 reduce-scatter.44
  1391.5 74.7 reduce-scatter.42
  1470.0 74.7 reduce-scatter.40
  1548.4 57.3 reduce-scatter.38
  1609.3 57.1 reduce-scatter.36
  1673.9 124.5 all-reduce.2
  1802.4 71.2 reduce-scatter.34
  1877.6 66.9 reduce-scatter.32
